TPU v7x, 32 devices: a whole 2x2x4 slice. The times are simulated.
32 devices in a mesh: groups: 2 (over x), tm: 8 (over z, y), space: 2 (over core).
Axes of the slice: x: 2, y: 2, z: 4, core: 2. Of those that a mesh axis runs over, the one named last changes fastest.
Arguments:
- latents: bfloat16 [32, 12, 80, 2240], P(('groups', 'tm'), 'space'), parts along dimension 0, may hold values from -8 to 8
- proj_weight: bfloat16 [2240, 3360], P('tm'), may hold values from -0.125 to 0.125
Outputs:
- attended: bfloat16 [32, 12, 80, 1120], P(('groups', 'tm'), 'space'), parts along dimension 0
There are 2 independent parts, one for each index of `groups`. A program takes and returns all parts, laid end to end along the dimension named above; an argument that names none is the same for every part. Nothing has to cross between parts.
All inputs are finite; a program needn't handle non-finite values.
Results may differ from a plain program's by a relative error of at most 0.0034.
Values may be sent and summed in bfloat16 or wider, within the bound.
A program may use at most 128 MiB of HBM per device.

v0:
```python
import jax
import jax.numpy as jnp
from jax import lax
from jax.sharding import PartitionSpec as P

HEADS = 10
HEAD = 112


def entering(value, axis, join, neutral):
    count, mine = (lax.axis_size(axis), lax.axis_index(axis))
    pieces = jax.tree.map(lambda part: lax.all_gather(part, axis), value)
    subtotal = jax.tree.map(
        lambda part, zero: jnp.full_like(part, 0) + jnp.asarray(zero, part.dtype), value, neutral
    )

    def hop(position, subtotal):
        longer = join(subtotal, jax.tree.map(lambda part: part[position], pieces))
        return jax.tree.map(lambda new, old: jnp.where(position < mine, new, old), longer, subtotal)

    return lax.fori_loop(0, count - 1, hop, subtotal)


def add_pairs(earlier, later):
    return (earlier[0] + later[0], earlier[1] + later[1])


def make_adder(flat, shard_rows):
    return jnp.dot(flat, shard_rows, preferred_element_type=jnp.float32)


def project_rows(flat, columns):
    return make_adder(flat, lax.all_gather(columns, "tm", axis=0, tiled=True))


def local_states(projected, heads_here):
    count = projected.shape[0]
    split = projected.astype(jnp.bfloat16).reshape(count, 3, heads_here, HEAD)
    queries = jax.nn.relu(split[:, 0])
    key_feats = jax.nn.relu(split[:, 1])
    values = split[:, 2]
    states = jnp.einsum("nhe,nhf->hef", key_feats, values, preferred_element_type=jnp.float32)
    key_sums = jnp.sum(key_feats, axis=0, dtype=jnp.float32)
    return (queries, states, key_sums)


def apply_states(queries, states, key_sums):
    numerator = jnp.einsum(
        "nhe,hef->nhf", queries, states.astype(jnp.bfloat16), preferred_element_type=jnp.float32
    )
    denominator = jnp.einsum(
        "nhe,he->nh", queries.astype(jnp.float32), key_sums, precision=lax.Precision.HIGHEST
    )
    return (numerator / (denominator[:, :, None] + 1.0)).astype(jnp.bfloat16)


def on_device(latents, proj_weight):
    frame_count, band_rows, column_count, channels = latents.shape
    shard_depth = proj_weight.shape[0]
    band_count = lax.axis_size("space")
    band_index = lax.axis_index("space")
    heads_here = HEADS // band_count
    grouped = proj_weight.reshape(shard_depth, 3, band_count, heads_here * HEAD)
    own_columns = lax.dynamic_index_in_dim(grouped, band_index, 2, keepdims=False)
    own_columns = own_columns.reshape(shard_depth, 3 * heads_here * HEAD)
    both_bands = lax.all_gather(latents, "space", axis=1, tiled=True)
    joined_rows = both_bands.shape[1]
    count = frame_count * joined_rows * column_count
    flat = both_bands.reshape(count, channels)
    projected = project_rows(flat, own_columns)
    queries, states, key_sums = local_states(projected, heads_here)
    identity = (jnp.zeros_like(states), jnp.zeros_like(key_sums))
    earlier = entering((states, key_sums), "tm", add_pairs, identity)
    attended = apply_states(queries, states + earlier[0], key_sums + earlier[1])
    attended = attended.reshape(frame_count, joined_rows, column_count, heads_here * HEAD)
    return lax.all_to_all(attended, "space", split_axis=1, concat_axis=3, tiled=True)


def solution(mesh):
    return jax.shard_map(
        on_device,
        mesh=mesh,
        in_specs=(P(("groups", "tm"), "space", None, None), P("tm", None)),
        out_specs=P(("groups", "tm"), "space", None, None),
        check_vma=False,
    )
```

profile of v0, /device:TPU:0, one launch (start us, length us, event | category | flops | bytes accessed | tf_op | source)
XLA Modules:
  0.0 274.9 jit_solution(16868224540163675632)
XLA Ops:
  6.5 0.0 all-gather.9.cloned.1.call-start
  6.5 0.7 all-gather.9.cloned.1.call-update
  7.3 0.0 all-gather.7.cloned.1.call-start
  7.3 5.4 %reshape.22 = bf16[280,3,2,560]{3,2,1,0:T(2,128)(2,1)S(1)} reshape(bf16[280,3360]{1,0:T(8,128)(2,1)} %param.5) | data formatting | bytes 3763200 | tf_op jit(solution)/shard_map/reshape | solution.py:63
  12.7 3.6 %constant_dynamic-slice_fusion = bf16[280,3,1,560]{3,2,1,0:T(2,128)(2,1)} fusion(bf16[280,3,2,560]{3,2,1,0:T(2,128)(2,1)S(1)} %reshape.22, s32[]{:T(128)S(6)} %select_n.42), kind=kLoop, calls=%fused_computation.21 | loop fusion | bytes 1881604 | tf_op jit(solution)/shard_map/jit(dynamic_index_in_dim)/dynamic_slice | solution.py:64
  16.3 6.2 %copy.25 = bf16[280,3,1,560]{0,3,1,2:T(8,128)(2,1)S(1)} copy(bf16[280,3,1,560]{3,2,1,0:T(2,128)(2,1)} %constant_dynamic-slice_fusion) | data formatting | bytes 1881600
  22.4 2.3 copy.13
  24.7 0.0 all-gather.7.cloned.1.call-update
  24.7 0.0 all-gather.11.cloned.1.call-start
  24.8 6.2 %all-gather.9.cloned.1.call-done = bf16[2,12,80,2240]{3,2,1,0:T(8,128)(2,1)} async-done(((bf16[2,6,80,2240]{3,2,1,0:T(8,128)(2,1)}), bf16[2,12,80,2240]{3,2,1,0:T(8,128)(2,1)}) %all-gather.9.cloned.1.call-update) | async-done | bytes 8601616 | tf_op jit(solution)/shard_map/all_gather | solution.py:66
  31.0 123.3 %all-gather.7.cloned.1.call-done = bf16[2240,1680]{1,0:T(8,128)(2,1)} async-done(((bf16[280,1680]{1,0:T(8,128)(2,1)}), bf16[2240,1680]{1,0:T(8,128)(2,1)}) %all-gather.7.cloned.1.call-update) | async-done | bytes 7526416 | tf_op jit(solution)/shard_map/all_gather | solution.py:33
  154.3 22.4 %convolution_convert_fusion = bf16[1680,1920]{1,0:T(8,128)(2,1)S(1)} fusion(bf16[2240,1680]{1,0:T(8,128)(2,1)} %all-gather.7.cloned.1.call-done, bf16[1920,2240]{1,0:T(8,128)(2,1)} %bitcast.54), kind=kOutput, calls=%fused_computation.2 | convolution fusion | flops 14453913600 | bytes 22579200 | tf_op jit(solution)/shard_map/dot_general | solution.py:29
  176.8 0.0 copy-start
  176.8 2.7 copy-done
  179.5 1.5 fusion.2
  181.0 0.0 all-gather.11.cloned.1.call-update
  181.0 2.1 convert_reduce_fusion
  183.1 31.0 %all-gather.2 = f32[8,5,112]{2,1,0:T(8,128)S(1)} all-gather(f32[1,5,112]{2,1,0:T(8,128)S(1)} %bitcast.53), channel_id=3, replica_groups=mesh['groups'=2,'tm'=8,'space'=2] {'tm'}, dimensions={0}, use_global_device_ids=true | all-gather | bytes 20160 | tf_op jit(solution)/shard_map/all_gather | solution.py:12
  214.1 16.5 %all-gather.11.cloned.1.call-done = f32[40,112,112]{2,1,0:T(8,128)} async-done(((f32[5,112,112]{2,1,0:T(8,128)}), f32[40,112,112]{2,1,0:T(8,128)}) %all-gather.11.cloned.1.call-update) | async-done | bytes 2007056 | tf_op jit(solution)/shard_map/all_gather | solution.py:12
  230.6 7.6 %while.16 = (s32[]{:T(128)}, f32[5,112,112]{2,1,0:T(8,128)S(1)}, f32[5,112]{1,0:T(8,128)S(1)}, s32[]{:T(128)}, f32[8,5,112,112]{3,2,1,0:T(8,128)}, /*index=5*/f32[8,5,112]{2,1,0:T(8,128)S(1)}, s32[]{:T(128)}, s32[]{:T(128)}) while((s32[]{:T(128)}, f32[5,112,112]{2,1,0:T(8,128)S(1)}, f32[5,112]{1,0:T(8,128)S(1)}, s32[]{:T(128)}, ...), condition=%wide.region_2.3_spmd.clone, body=%wide.region_1.2_spmd.clone.sunk | while | flops 189844 | bytes 759475 | solution.py:21
  230.6 1.0 add_select_fusion.4
  231.7 1.0 add_select_fusion.4
  232.8 1.0 add_select_fusion.4
  233.9 1.0 add_select_fusion.4
  235.0 1.0 add_select_fusion.4
  236.1 1.0 add_select_fusion.4
  237.1 1.0 add_select_fusion.4
  238.2 0.0 copy-start.1
  238.2 2.6 fusion.5
  240.9 0.0 copy-done.1
  240.9 2.4 fusion
  243.3 8.0 %reshape.34 = bf16[2,12,80,560]{2,1,0,3:T(8,128)(2,1)} reshape(bf16[1920,5,112]{0,2,1:T(8,128)(2,1)S(1)} %fusion) | data formatting | bytes 4300800 | tf_op jit(solution)/shard_map/reshape | solution.py:75
  251.4 6.0 %copy.16 = bf16[2,12,80,560]{3,2,0,1:T(8,128)(2,1)S(1)} copy(bf16[2,12,80,560]{2,1,0,3:T(8,128)(2,1)} %reshape.34) | data formatting | bytes 4300800 | tf_op jit(solution)/shard_map/reshape | solution.py:75
  257.3 5.7 %all_to_all.18 = bf16[2,12,80,560]{3,2,0,1:T(8,128)(2,1)S(1)} all-to-all(bf16[2,12,80,560]{3,2,0,1:T(8,128)(2,1)S(1)} %copy.16), channel_id=1, replica_groups=mesh['groups'=2,'tm'=8,'space'=2] {'space'}, dimensions={1} | all-to-all | bytes 4300800 | tf_op jit(solution)/shard_map/all_to_all | solution.py:76
  263.0 2.5 copy.18
  265.6 2.9 %all_to_all.16 = bf16[2,6,80,1120]{3,2,1,0:T(8,128)(2,1)} reshape(bf16[2,6,80,2,560]{4,3,2,1,0:T(2,128)(2,1)S(1)} %copy.18) | data formatting | bytes 4300800 | tf_op jit(solution)/shard_map/all_to_all | solution.py:76
  (11 shorter events, 0.1 us)
Async XLA Ops:
  6.5 24.5 %all-gather.9.cloned.1.call-start = ((), (), s32[]{:S(2)}) async-start(), calls=%async_computation.2 | async-start | bytes 13271040 | tf_op jit(solution)/shard_map/all_gather | solution.py:66
  7.3 147.1 %all-gather.7.cloned.1.call-start = ((), (), s32[]{:S(2)}) async-start(), calls=%async_computation.1 | async-start | bytes 9031680 | tf_op jit(solution)/shard_map/all_gather | solution.py:33
  24.7 205.9 %all-gather.11.cloned.1.call-start = ((), (), s32[]{:S(2)}) async-start(), calls=%async_computation.3 | async-start | bytes 2580480 | tf_op jit(solution)/shard_map/all_gather | solution.py:12
  176.8 2.7 copy-start
  238.2 2.7 copy-start.1
Sparse Core Ops, SparseCore 0:
  8.9 22.1 all-gather.8
  33.2 121.0 all-gather.6
  181.1 49.4 all-gather.10
where the time goes:
time: 276 us; the launch traced here: 275 us
  waiting for transfers between devices  147 us (53%)
  local copies, waits for them, and re-layouts  39.5 us (14%)
  blocking collectives  36.7 us (13%)
  matrix products  28.9 us (10%)
  between operations  13.2 us (5%)
  other arithmetic  9.53 us (3%)
    all_gather x1, waiting for transfers between devices, project_rows(): return make_adder(flat, lax.all_gather(columns, 'tm', axis=0, tiled=True))  123 us
    all_gather x1, blocking collectives, entering(): pieces = jax.tree.map(lambda part: lax.all_gather(part, axis), value)  31 us
    dot_general x1, matrix products, make_adder(): return jnp.dot(flat, shard_rows, preferred_element_type=jnp.float32)  22.4 us
    all_gather x1, waiting for transfers between devices, entering(): pieces = jax.tree.map(lambda part: lax.all_gather(part, axis), value)  16.5 us
    reshape x2, local copies, waits for them, and re-layouts, on_device(): attended.reshape(frame_count, joined_rows, column_count, heads_here * HEAD)  14 us
    unnamed x5, local copies, waits for them, and re-layouts  8.87 us
    select_n x14, other arithmetic, hop(): jnp.where(position < mine, new, old)  7.4 us
    all_gather x1, waiting for transfers between devices, on_device(): both_bands = lax.all_gather(latents, 'space', axis=1, tiled=True)  6.23 us
  transfers between devices with their start and end apart: 3, of which 3 were waited for; matrix products, arithmetic and copies ran while one was open for 7% of the time, Pallas kernels for 0%

commit v1 on v0

--- a/solution.py
+++ b/solution.py
@@ -5,6 +5,18 @@
 
 HEADS = 10
 HEAD = 112
+
+
+def ring_gather(shard, axis, dim):
+    ways, here, step = (lax.axis_size(axis), lax.axis_index(axis), shard.shape[dim])
+    shape = [n * ways if d == dim else n for d, n in enumerate(shard.shape)]
+    full = lax.dynamic_update_slice_in_dim(
+        jnp.zeros(shape, shard.dtype), shard, here * step, axis=dim
+    )
+    for far in range(1, ways):
+        shard = lax.ppermute(shard, axis, [(d, (d + 1) % ways) for d in range(ways)])
+        full = lax.dynamic_update_slice_in_dim(full, shard, (here - far) % ways * step, axis=dim)
+    return full
 
 
 def entering(value, axis, join, neutral):
@@ -30,7 +42,7 @@
 
 
 def project_rows(flat, columns):
-    return make_adder(flat, lax.all_gather(columns, "tm", axis=0, tiled=True))
+    return make_adder(flat, ring_gather(columns, "tm", 0))
 
 
 def local_states(projected, heads_here):

time: 276 us -> 428 us (1.55)
  local copies, waits for them, and re-layouts: 39.5 us -> 167 us
  waiting for transfers between devices: 147 us -> 167 us
    ppermute x0 -> x7, waiting for transfers between devices: none -> 147 us  [ring_gather(): lax.ppermute(shard, axis, [(d, (d + 1) % ways) for d in range(ways)])]
    all_gather x1 -> x0, waiting for transfers between devices: 123 us -> none  [project_rows(): return make_adder(flat, lax.all_gather(columns, 'tm', axis=0, tiled=True))]
    dynamic_update_slice x0 -> x8, local copies, waits for them, and re-layouts: none -> 108 us  [the longest x7 95.9 us: ring_gather(): lax.dynamic_update_slice_in_dim(full, shard, (here - far) % ways * step,...]
    ppermute x0 -> x7, local copies, waits for them, and re-layouts: none -> 13.3 us  [ring_gather(): lax.ppermute(shard, axis, [(d, (d + 1) % ways) for d in range(ways)])]
    all_gather x1, waiting for transfers between devices: 6.23 us -> 0.01 us  [on_device(): both_bands = lax.all_gather(latents, 'space', axis=1, tiled=True)]
    unnamed x5 -> x17, local copies, waits for them, and re-layouts: 8.87 us -> 11.7 us
  transfers between devices with their start and end apart: 3 -> 9, of which waited for: 3 -> 7; matrix products, arithmetic and copies ran while one was open for 7% -> 34% of each run, Pallas kernels for 0% -> 0%
where the time goes in v1:
time: 428 us; the launch traced here: 424 us
  waiting for transfers between devices  167 us (39%)
  local copies, waits for them, and re-layouts  167 us (39%)
  blocking collectives  36.9 us (9%)
  matrix products  27.3 us (6%)
  between operations  13.6 us (3%)
  other arithmetic  9.53 us (2%)
    ppermute x7, waiting for transfers between devices, ring_gather(): lax.ppermute(shard, axis, [(d, (d + 1) % ways) for d in range(ways)])  147 us
    dynamic_update_slice x7, local copies, waits for them, and re-layouts, ring_gather(): lax.dynamic_update_slice_in_dim(full, shard, (here - far) % ways * step,...  95.9 us
    all_gather x1, blocking collectives, entering(): pieces = jax.tree.map(lambda part: lax.all_gather(part, axis), value)  31.2 us
    dot_general x1, matrix products, make_adder(): return jnp.dot(flat, shard_rows, preferred_element_type=jnp.float32)  20.8 us
    all_gather x1, waiting for transfers between devices, entering(): pieces = jax.tree.map(lambda part: lax.all_gather(part, axis), value)  18.3 us
    reshape x2, local copies, waits for them, and re-layouts, on_device(): attended.reshape(frame_count, joined_rows, column_count, heads_here * HEAD)  14 us
    ppermute x7, local copies, waits for them, and re-layouts, ring_gather(): lax.ppermute(shard, axis, [(d, (d + 1) % ways) for d in range(ways)])  13.3 us
    dynamic_update_slice x1, local copies, waits for them, and re-layouts, ring_gather(): lax.dynamic_update_slice_in_dim(jnp.zeros(shape, shard.dtype), shard, her...  12.4 us
  transfers between devices with their start and end apart: 9, of which 7 were waited for; matrix products, arithmetic and copies ran while one was open for 34% of the time, Pallas kernels for 0%

profile of v1, /device:TPU:0, one launch (start us, length us, event | category | flops | bytes accessed | tf_op | source)
XLA Modules:
  0.0 424.1 jit_solution(4813444243621213190)
XLA Ops:
  6.5 0.0 all-gather.6.cloned.1.call-start
  6.5 0.7 all-gather.6.cloned.1.call-update
  7.3 0.0 all-gather.8.cloned.1.call-start
  7.3 5.4 %reshape.22 = bf16[280,3,2,560]{3,2,1,0:T(2,128)(2,1)S(1)} reshape(bf16[280,3360]{1,0:T(8,128)(2,1)} %param.5) | data formatting | bytes 3763200 | tf_op jit(solution)/shard_map/reshape | solution.py:75
  12.7 3.6 constant_dynamic-slice_fusion
  16.3 6.2 %copy.32 = bf16[280,3,1,560]{0,3,1,2:T(8,128)(2,1)S(1)} copy(bf16[280,3,1,560]{3,2,1,0:T(2,128)(2,1)} %constant_dynamic-slice_fusion) | data formatting | bytes 1881600
  22.4 1.6 copy.13
  24.0 3.1 collective-permute-start
  27.1 25.2 %collective-permute-done = bf16[280,1680]{1,0:T(8,128)(2,1)S(1)} collective-permute-done((bf16[280,1680]{1,0:T(8,128)(2,1)S(1)}, bf16[280,1680]{1,0:T(8,128)(2,1)S(1)}, u32[]{:S(2)}, u32[]{:S(2)}) %collective-permute-start) | collective-permute-done | bytes 940832 | tf_op jit(solution)/shard_map/ppermute | solution.py:17
  52.4 0.0 collective-permute-start.1
  52.4 26.1 %collective-permute-done.1 = bf16[280,1680]{1,0:T(8,128)(2,1)S(1)} collective-permute-done((bf16[280,1680]{1,0:T(8,128)(2,1)S(1)}, bf16[280,1680]{1,0:T(8,128)(2,1)S(1)}, u32[]{:S(2)}, u32[]{:S(2)}) %collective-permute-start.1) | collective-permute-done | bytes 940832 | tf_op jit(solution)/shard_map/ppermute | solution.py:17
  78.5 0.0 collective-permute-start.2
  78.5 25.3 %collective-permute-done.2 = bf16[280,1680]{1,0:T(8,128)(2,1)S(1)} collective-permute-done((bf16[280,1680]{1,0:T(8,128)(2,1)S(1)}, bf16[280,1680]{1,0:T(8,128)(2,1)S(1)}, u32[]{:S(2)}, u32[]{:S(2)}) %collective-permute-start.2) | collective-permute-done | bytes 940832 | tf_op jit(solution)/shard_map/ppermute | solution.py:17
  103.8 0.9 copy-done
  104.8 0.0 collective-permute-start.3
  104.8 24.4 %collective-permute-done.3 = bf16[280,1680]{1,0:T(8,128)(2,1)S(1)} collective-permute-done((bf16[280,1680]{1,0:T(8,128)(2,1)S(1)}, bf16[280,1680]{1,0:T(8,128)(2,1)S(1)}, u32[]{:S(2)}, u32[]{:S(2)}) %collective-permute-start.3) | collective-permute-done | bytes 940832 | tf_op jit(solution)/shard_map/ppermute | solution.py:17
  129.2 1.0 copy-done.2
  130.2 0.0 collective-permute-start.4
  130.2 23.6 %collective-permute-done.4 = bf16[280,1680]{1,0:T(8,128)(2,1)S(1)} collective-permute-done((bf16[280,1680]{1,0:T(8,128)(2,1)S(1)}, bf16[280,1680]{1,0:T(8,128)(2,1)S(1)}, u32[]{:S(2)}, u32[]{:S(2)}) %collective-permute-start.4) | collective-permute-done | bytes 940832 | tf_op jit(solution)/shard_map/ppermute | solution.py:17
  153.7 1.0 copy-done.4
  154.7 0.0 collective-permute-start.5
  154.7 22.8 %collective-permute-done.5 = bf16[280,1680]{1,0:T(8,128)(2,1)} collective-permute-done((bf16[280,1680]{1,0:T(8,128)(2,1)S(1)}, bf16[280,1680]{1,0:T(8,128)(2,1)}, u32[]{:S(2)}, u32[]{:S(2)}) %collective-permute-start.5) | collective-permute-done | bytes 940832 | tf_op jit(solution)/shard_map/ppermute | solution.py:17
  177.5 0.0 collective-permute-start.6
  177.5 3.5 broadcast_in_dim.10
  181.1 12.4 %dynamic_update_slice.24 = bf16[2240,1680]{0,1:T(8,128)(2,1)} dynamic-update-slice(bf16[2240,1680]{0,1:T(8,128)(2,1)} %broadcast_in_dim.10, bf16[280,1680]{0,1:T(8,128)(2,1)S(1)} %bitcast.47, s32[]{:T(128)S(6)} %select_n.98, s32[]{:T(128)} %constant.92.clone.1) | dynamic-update-slice | bytes 1881604 | tf_op jit(solution)/shard_map/dynamic_update_slice | solution.py:13
  193.5 1.6 copy.14
  195.1 13.1 %dynamic_update_slice.25 = bf16[2240,1680]{0,1:T(8,128)(2,1)} dynamic-update-slice(bf16[2240,1680]{0,1:T(8,128)(2,1)} %dynamic_update_slice.24, bf16[280,1680]{0,1:T(8,128)(2,1)S(1)} %copy.14, s32[]{:T(128)S(6)} %select_n.100, s32[]{:T(128)} %constant.92.clone.1) | dynamic-update-slice | bytes 1881604 | tf_op jit(solution)/shard_map/dynamic_update_slice | solution.py:18
  208.2 1.6 copy.15
  209.9 13.6 %dynamic_update_slice.26 = bf16[2240,1680]{0,1:T(8,128)(2,1)} dynamic-update-slice(bf16[2240,1680]{0,1:T(8,128)(2,1)} %dynamic_update_slice.25, bf16[280,1680]{0,1:T(8,128)(2,1)S(1)} %copy.15, s32[]{:T(128)S(6)} %select_n.102, s32[]{:T(128)} %constant.92.clone.1) | dynamic-update-slice | bytes 1881604 | tf_op jit(solution)/shard_map/dynamic_update_slice | solution.py:18
  223.5 0.0 copy-done.1
  223.5 1.6 copy.16
  225.2 13.8 %dynamic_update_slice.27 = bf16[2240,1680]{0,1:T(8,128)(2,1)} dynamic-update-slice(bf16[2240,1680]{0,1:T(8,128)(2,1)} %dynamic_update_slice.26, bf16[280,1680]{0,1:T(8,128)(2,1)S(1)} %copy.16, s32[]{:T(128)S(6)} %select_n.104, s32[]{:T(128)} %constant.92.clone.1) | dynamic-update-slice | bytes 1881604 | tf_op jit(solution)/shard_map/dynamic_update_slice | solution.py:18
  239.0 1.6 copy.17
  240.6 13.8 %dynamic_update_slice.28 = bf16[2240,1680]{0,1:T(8,128)(2,1)} dynamic-update-slice(bf16[2240,1680]{0,1:T(8,128)(2,1)} %dynamic_update_slice.27, bf16[280,1680]{0,1:T(8,128)(2,1)S(1)} %copy.17, s32[]{:T(128)S(6)} %select_n.106, s32[]{:T(128)} %constant.92.clone.1) | dynamic-update-slice | bytes 1881604 | tf_op jit(solution)/shard_map/dynamic_update_slice | solution.py:18
  254.4 1.6 copy.18
  256.1 13.8 %dynamic_update_slice.29 = bf16[2240,1680]{0,1:T(8,128)(2,1)} dynamic-update-slice(bf16[2240,1680]{0,1:T(8,128)(2,1)} %dynamic_update_slice.28, bf16[280,1680]{0,1:T(8,128)(2,1)S(1)} %copy.18, s32[]{:T(128)S(6)} %select_n.108, s32[]{:T(128)} %constant.92.clone.1) | dynamic-update-slice | bytes 1881604 | tf_op jit(solution)/shard_map/dynamic_update_slice | solution.py:18
  269.9 2.6 copy.19
  272.5 13.8 %dynamic_update_slice.30 = bf16[2240,1680]{0,1:T(8,128)(2,1)} dynamic-update-slice(bf16[2240,1680]{0,1:T(8,128)(2,1)} %dynamic_update_slice.29, bf16[280,1680]{0,1:T(8,128)(2,1)S(1)} %copy.19, s32[]{:T(128)S(6)} %select_n.110, s32[]{:T(128)} %constant.92.clone.1) | dynamic-update-slice | bytes 1881604 | tf_op jit(solution)/shard_map/dynamic_update_slice | solution.py:18
  286.4 0.0 collective-permute-done.6
  286.4 2.6 copy.20
  288.9 13.8 %dynamic_update_slice.31 = bf16[2240,1680]{0,1:T(8,128)(2,1)} dynamic-update-slice(bf16[2240,1680]{0,1:T(8,128)(2,1)} %dynamic_update_slice.30, bf16[280,1680]{0,1:T(8,128)(2,1)S(1)} %copy.20, s32[]{:T(128)S(6)} %select_n.112, s32[]{:T(128)} %constant.92.clone.1) | dynamic-update-slice | bytes 1881604 | tf_op jit(solution)/shard_map/dynamic_update_slice | solution.py:18
  302.8 20.8 %convolution_convert_fusion = bf16[1680,1920]{1,0:T(8,128)(2,1)S(1)} fusion(bf16[2240,1680]{0,1:T(8,128)(2,1)} %dynamic_update_slice.31, bf16[1920,2240]{1,0:T(8,128)(2,1)} %bitcast.55), kind=kOutput, calls=%fused_computation.2 | convolution fusion | flops 14453913600 | bytes 22579200 | tf_op jit(solution)/shard_map/dot_general | solution.py:41
  323.6 2.7 copy-done.6
  326.3 1.5 fusion.2
  327.7 0.0 all-gather.8.cloned.1.call-update
  327.8 2.1 convert_reduce_fusion
  329.9 31.2 %all-gather.2 = f32[8,5,112]{2,1,0:T(8,128)S(1)} all-gather(f32[1,5,112]{2,1,0:T(8,128)S(1)} %bitcast.54), channel_id=3, replica_groups=mesh['groups'=2,'tm'=8,'space'=2] {'tm'}, dimensions={0}, use_global_device_ids=true | all-gather | bytes 20160 | tf_op jit(solution)/shard_map/all_gather | solution.py:24
  361.1 18.3 %all-gather.8.cloned.1.call-done = f32[40,112,112]{2,1,0:T(8,128)} async-done(((f32[5,112,112]{2,1,0:T(8,128)}), f32[40,112,112]{2,1,0:T(8,128)}) %all-gather.8.cloned.1.call-update) | async-done | bytes 2007056 | tf_op jit(solution)/shard_map/all_gather | solution.py:24
  379.4 7.6 %while.16 = (s32[]{:T(128)}, f32[5,112,112]{2,1,0:T(8,128)S(1)}, f32[5,112]{1,0:T(8,128)S(1)}, s32[]{:T(128)}, f32[8,5,112,112]{3,2,1,0:T(8,128)}, /*index=5*/f32[8,5,112]{2,1,0:T(8,128)S(1)}, s32[]{:T(128)}, s32[]{:T(128)}) while((s32[]{:T(128)}, f32[5,112,112]{2,1,0:T(8,128)S(1)}, f32[5,112]{1,0:T(8,128)S(1)}, s32[]{:T(128)}, ...), condition=%wide.region_2.3_spmd.clone, body=%wide.region_1.2_spmd.clone.sunk | while | flops 189844 | bytes 759475 | solution.py:33
  379.4 1.0 add_select_fusion.4
  380.5 1.0 add_select_fusion.4
  381.6 1.0 add_select_fusion.4
  382.7 1.0 add_select_fusion.4
  383.7 1.0 add_select_fusion.4
  384.8 1.0 add_select_fusion.4
  385.9 1.0 add_select_fusion.4
  387.0 0.0 copy-start.7
  387.0 2.6 fusion.5
  389.7 2.4 fusion
  392.1 8.1 %reshape.34 = bf16[2,12,80,560]{2,1,0,3:T(8,128)(2,1)} reshape(bf16[1920,5,112]{0,2,1:T(8,128)(2,1)S(1)} %fusion) | data formatting | bytes 4300800 | tf_op jit(solution)/shard_map/reshape | solution.py:87
  400.2 6.0 %copy.23 = bf16[2,12,80,560]{3,2,0,1:T(8,128)(2,1)S(1)} copy(bf16[2,12,80,560]{2,1,0,3:T(8,128)(2,1)} %reshape.34) | data formatting | bytes 4300800 | tf_op jit(solution)/shard_map/reshape | solution.py:87
  406.1 5.7 %all_to_all.18 = bf16[2,12,80,560]{3,2,0,1:T(8,128)(2,1)S(1)} all-to-all(bf16[2,12,80,560]{3,2,0,1:T(8,128)(2,1)S(1)} %copy.23), channel_id=1, replica_groups=mesh['groups'=2,'tm'=8,'space'=2] {'space'}, dimensions={1} | all-to-all | bytes 4300800 | tf_op jit(solution)/shard_map/all_to_all | solution.py:88
  411.8 2.5 copy.25
  414.4 2.9 all_to_all.16
  (22 shorter events, 0.1 us)
Async XLA Ops:
  6.5 296.2 %all-gather.6.cloned.1.call-start = ((), (), s32[]{:S(2)}) async-start(), calls=%async_computation.1 | async-start | bytes 13271040 | tf_op jit(solution)/shard_map/all_gather | solution.py:78
  7.3 372.1 %all-gather.8.cloned.1.call-start = ((), (), s32[]{:S(2)}) async-start(), calls=%async_computation.2 | async-start | bytes 2580480 | tf_op jit(solution)/shard_map/all_gather | solution.py:24
  24.0 28.4 %collective-permute-start = (bf16[280,1680]{1,0:T(8,128)(2,1)S(1)}, bf16[280,1680]{1,0:T(8,128)(2,1)S(1)}, u32[]{:S(2)}, u32[]{:S(2)}) collective-permute-start(bf16[280,1680]{1,0:T(8,128)(2,1)S(1)} %copy.13), channel_id=1, source_target_pairs={{0,2},{2,4},{4,6},{6,8},{8,10},{10,12},{12,14},{14,0},{1,3},{3,5},... | collective-permute-start | bytes 2822408 | tf_op jit(solution)/shard_map/ppermute | solution.py:17
  52.4 26.1 %collective-permute-start.1 = (bf16[280,1680]{1,0:T(8,128)(2,1)S(1)}, bf16[280,1680]{1,0:T(8,128)(2,1)S(1)}, u32[]{:S(2)}, u32[]{:S(2)}) collective-permute-start(bf16[280,1680]{1,0:T(8,128)(2,1)S(1)} %collective-permute-done), channel_id=1, source_target_pairs={{0,2},{2,4},{4,6},{6,8},{8,10},{10,12},{12,14},{14,0},{1,3},{3,5},... | collective-permute-start | bytes 2822408 | tf_op jit(solution)/shard_map/ppermute | solution.py:17
  78.5 25.3 %collective-permute-start.2 = (bf16[280,1680]{1,0:T(8,128)(2,1)S(1)}, bf16[280,1680]{1,0:T(8,128)(2,1)S(1)}, u32[]{:S(2)}, u32[]{:S(2)}) collective-permute-start(bf16[280,1680]{1,0:T(8,128)(2,1)S(1)} %collective-permute-done.1), channel_id=1, source_target_pairs={{0,2},{2,4},{4,6},{6,8},{8,10},{10,12},{12,14},{14,0},{1,3},{3,5},... | collective-permute-start | bytes 2822408 | tf_op jit(solution)/shard_map/ppermute | solution.py:17
  103.8 1.0 copy-start
  104.8 24.4 %collective-permute-start.3 = (bf16[280,1680]{1,0:T(8,128)(2,1)S(1)}, bf16[280,1680]{1,0:T(8,128)(2,1)S(1)}, u32[]{:S(2)}, u32[]{:S(2)}) collective-permute-start(bf16[280,1680]{1,0:T(8,128)(2,1)S(1)} %collective-permute-done.2), channel_id=1, source_target_pairs={{0,2},{2,4},{4,6},{6,8},{8,10},{10,12},{12,14},{14,0},{1,3},{3,5},... | collective-permute-start | bytes 2822408 | tf_op jit(solution)/shard_map/ppermute | solution.py:17
  129.2 1.0 copy-start.2
  130.2 23.6 %collective-permute-start.4 = (bf16[280,1680]{1,0:T(8,128)(2,1)S(1)}, bf16[280,1680]{1,0:T(8,128)(2,1)S(1)}, u32[]{:S(2)}, u32[]{:S(2)}) collective-permute-start(bf16[280,1680]{1,0:T(8,128)(2,1)S(1)} %collective-permute-done.3), channel_id=1, source_target_pairs={{0,2},{2,4},{4,6},{6,8},{8,10},{10,12},{12,14},{14,0},{1,3},{3,5},... | collective-permute-start | bytes 2822408 | tf_op jit(solution)/shard_map/ppermute | solution.py:17
  153.7 1.0 copy-start.4
  154.7 22.8 %collective-permute-start.5 = (bf16[280,1680]{1,0:T(8,128)(2,1)S(1)}, bf16[280,1680]{1,0:T(8,128)(2,1)}, u32[]{:S(2)}, u32[]{:S(2)}) collective-permute-start(bf16[280,1680]{1,0:T(8,128)(2,1)S(1)} %collective-permute-done.4), channel_id=1, source_target_pairs={{0,2},{2,4},{4,6},{6,8},{8,10},{10,12},{12,14},{14,0},{1,3},{3,5},... | collective-permute-start | bytes 2822408 | tf_op jit(solution)/shard_map/ppermute | solution.py:17
  177.5 108.8 %collective-permute-start.6 = (bf16[280,1680]{1,0:T(8,128)(2,1)}, bf16[280,1680]{1,0:T(8,128)(2,1)}, u32[]{:S(2)}, u32[]{:S(2)}) collective-permute-start(bf16[280,1680]{1,0:T(8,128)(2,1)} %collective-permute-done.5), channel_id=1, source_target_pairs={{0,2},{2,4},{4,6},{6,8},{8,10},{10,12},{12,14},{14,0},{1,3},{3,5},... | collective-permute-start | bytes 2822408 | tf_op jit(solution)/shard_map/ppermute | solution.py:17
  208.2 15.3 %copy-start.1 = (bf16[280,1680]{1,0:T(8,128)(2,1)S(1)}, bf16[280,1680]{1,0:T(8,128)(2,1)}, u32[]{:S(2)}) copy-start(bf16[280,1680]{1,0:T(8,128)(2,1)} %copy-done) | copy-start | bytes 2822404
  223.5 15.5 %copy-start.3 = (bf16[280,1680]{1,0:T(8,128)(2,1)S(1)}, bf16[280,1680]{1,0:T(8,128)(2,1)}, u32[]{:S(2)}) copy-start(bf16[280,1680]{1,0:T(8,128)(2,1)} %copy-done.2) | copy-start | bytes 2822404
  239.0 15.5 %copy-start.5 = (bf16[280,1680]{1,0:T(8,128)(2,1)S(1)}, bf16[280,1680]{1,0:T(8,128)(2,1)}, u32[]{:S(2)}) copy-start(bf16[280,1680]{1,0:T(8,128)(2,1)} %copy-done.4) | copy-start | bytes 2822404
  323.6 2.7 copy-start.6
  387.0 2.7 copy-start.7
Sparse Core Ops, SparseCore 0:
  8.9 22.1 all-gather.5
  327.9 51.4 all-gather.7
